TPU v7x, 32 devices: a whole 2x2x4 slice. The times are simulated.
32 devices in a mesh: dp: 8 (over z, x), seq: 4 (over y, core).
Axes of the slice: x: 2, y: 2, z: 4, core: 2. Of those that a mesh axis runs over, the one named last changes fastest.
Arguments:
- inputs: bfloat16 [8, 2048, 768], P('dp', 'seq'), may hold values from -2.5 to 2.5
- cotangent: bfloat16 [8, 2048, 768], P('dp', 'seq'), may hold values from -6 to 6
- qkv_weight: float32 [768, 2304], P('seq', 'dp'), may hold values from -0.21875 to 0.21875
- qkv_first: float32 [768, 2304], P('seq', 'dp'), may hold values from -128 to 128
- qkv_second: float32 [768, 2304], P('seq', 'dp'), may hold values from 491.52 to 4096
- out_weight: float32 [768, 768], P('seq', 'dp'), may hold values from -2.5 to 2.5
- out_first: float32 [768, 768], P('seq', 'dp'), may hold values from -13.57645 to 13.57645
- out_second: float32 [768, 768], P('seq', 'dp'), may hold values from 5.76 to 46.08
- fc_weight: float32 [768, 3072], P('seq', 'dp'), may hold values from -0.21875 to 0.21875
- fc_first: float32 [768, 3072], P('seq', 'dp'), may hold values from -46.08 to 46.08
- fc_second: float32 [768, 3072], P('seq', 'dp'), may hold values from 65.536 to 524.288
- proj_weight: float32 [3072, 768], P('seq', 'dp'), may hold values from -0.109375 to 0.109375
- proj_first: float32 [3072, 768], P('seq', 'dp'), may hold values from -97.28 to 97.28
- proj_second: float32 [3072, 768], P('seq', 'dp'), may hold values from 294.912 to 2359.296
- vectors: float32 [12, 768], P('seq', 'dp'), may hold values from -0.4 to 1.4, as said below
- vector_first: float32 [12, 768], P('seq', 'dp'), may hold values from -128 to 128
- vector_second: float32 [12, 768], P('seq', 'dp'), may hold values from 327.68 to 4096
Outputs:
- outputs: bfloat16 [8, 2048, 768], P('dp', 'seq')
- input_grad: bfloat16 [8, 2048, 768], P('dp', 'seq')
- qkv_first_new: float32 [768, 2304], P('seq', 'dp')
- qkv_second_new: float32 [768, 2304], P('seq', 'dp')
- qkv_updated: float32 [768, 2304], P('seq', 'dp')
- qkv_lowered: bfloat16 [768, 2304], P('seq', 'dp')
- out_first_new: float32 [768, 768], P('seq', 'dp')
- out_second_new: float32 [768, 768], P('seq', 'dp')
- out_updated: float32 [768, 768], P('seq', 'dp')
- out_lowered: bfloat16 [768, 768], P('seq', 'dp')
- fc_first_new: float32 [768, 3072], P('seq', 'dp')
- fc_second_new: float32 [768, 3072], P('seq', 'dp')
- fc_updated: float32 [768, 3072], P('seq', 'dp')
- fc_lowered: bfloat16 [768, 3072], P('seq', 'dp')
- proj_first_new: float32 [3072, 768], P('seq', 'dp')
- proj_second_new: float32 [3072, 768], P('seq', 'dp')
- proj_updated: float32 [3072, 768], P('seq', 'dp')
- proj_lowered: bfloat16 [3072, 768], P('seq', 'dp')
- vector_first_new: float32 [12, 768], P('seq', 'dp')
- vector_second_new: float32 [12, 768], P('seq', 'dp')
- vector_updated: float32 [12, 768], P('seq', 'dp')
- vector_lowered: bfloat16 [12, 768], P('seq', 'dp')
Inputs may be any that keep to these rules, and one draw needn't show every extreme that they name: `vectors`: rows 0 and 5 are LayerNorm gains near one, the other rows are biases of order a tenth.
All inputs are finite; a program needn't handle non-finite values.
Results may differ from a plain program's by a relative error of at most 0.018.
Values may be sent and summed in bfloat16 or wider, within the bound.
No kernel may reach another device: no remote copies, remote signals or barrier semaphores. Data moves between devices by JAX's collectives and lax.ppermute only.
A program may use at most 192 MiB of HBM per device.

v0:
```python
import jax
import jax.numpy as jnp
from jax import lax
from jax.sharding import PartitionSpec as P

D = 768
HEADS = 12
HEAD_DIM = 64
FF = 3072
DEPTH = 12
LEN = 2048
STEP = 10
beta_one = 0.5
beta_two = 0.5
matrix_decay = 0.1


def layer_norm(values, gain, shift):
    centre = values - jnp.mean(values, -1, keepdims=True)
    spread = jnp.mean(centre * centre, -1, keepdims=True)
    return centre * lax.rsqrt(spread + 1e-05) * gain + shift


def gelu_tanh(values):
    return jax.nn.gelu(values, approximate=True)


def adam_update(master, first, second, grad, rate, decay):
    first_new = beta_one * first + (1.0 - beta_one) * grad
    second_new = beta_two * second + (1.0 - beta_two) * grad * grad
    fix_one = 1.0 - beta_one**STEP
    fix_two = 1.0 - beta_two**STEP
    direction = first_new / fix_one / (jnp.sqrt(second_new / fix_two) + 1e-08)
    updated = master - rate * (direction + decay * master)
    return (first_new, second_new, updated, updated.astype(jnp.bfloat16))


def attend_forward(query_all, key_all, value_all):
    head_count, seq_len, head_width = query_all.shape
    block_len = min(512, seq_len)
    block_count = seq_len // block_len
    score_scale = head_width ** (-0.5)
    key_pos = jnp.arange(seq_len)[None, None, :]

    def one_block(block_index):
        block_start = block_index * block_len
        query_blk = lax.dynamic_slice_in_dim(query_all, block_start, block_len, 1)
        scores = (
            jnp.einsum("gqd,gkd->gqk", query_blk, key_all, preferred_element_type=jnp.float32)
            * score_scale
        )
        query_pos = block_start + jnp.arange(block_len)[None, :, None]
        scores = jnp.where(key_pos <= query_pos, scores, -1e30)
        row_max = jnp.max(scores, -1, keepdims=True)
        exponent = jnp.exp(scores - row_max)
        row_total = jnp.sum(exponent, -1, keepdims=True)
        attn_probs = (exponent / row_total).astype(jnp.bfloat16)
        block_out = jnp.einsum(
            "gqk,gkd->gqd", attn_probs, value_all, preferred_element_type=jnp.float32
        )
        return (block_out.astype(jnp.bfloat16), row_max + jnp.log(row_total))

    block_out, log_total = lax.map(one_block, jnp.arange(block_count))
    block_out = block_out.transpose(1, 0, 2, 3).reshape(head_count, seq_len, head_width)
    log_total = log_total.transpose(1, 0, 2, 3).reshape(head_count, seq_len, 1)
    return (block_out, log_total)


def attend_backward(query_all, key_all, value_all, grad_all, log_total):
    head_count, seq_len, head_width = query_all.shape
    block_len = min(512, seq_len)
    block_count = seq_len // block_len
    score_scale = head_width ** (-0.5)
    key_pos = jnp.arange(seq_len)[None, None, :]

    def one_block(carry, block_index):
        key_grad, value_grad = carry
        block_start = block_index * block_len
        query_blk = lax.dynamic_slice_in_dim(query_all, block_start, block_len, 1)
        grad_blk = lax.dynamic_slice_in_dim(grad_all, block_start, block_len, 1)
        total_blk = lax.dynamic_slice_in_dim(log_total, block_start, block_len, 1)
        scores = (
            jnp.einsum("gqd,gkd->gqk", query_blk, key_all, preferred_element_type=jnp.float32)
            * score_scale
        )
        query_pos = block_start + jnp.arange(block_len)[None, :, None]
        scores = jnp.where(key_pos <= query_pos, scores, -1e30)
        attn_probs = jnp.exp(scores - total_blk)
        grad_probs = jnp.einsum(
            "gqd,gkd->gqk", grad_blk, value_all, preferred_element_type=jnp.float32
        )
        inner = jnp.sum(attn_probs * grad_probs, -1, keepdims=True)
        grad_scores = (attn_probs * (grad_probs - inner)).astype(jnp.bfloat16)
        query_grad = (
            jnp.einsum("gqk,gkd->gqd", grad_scores, key_all, preferred_element_type=jnp.float32)
            * score_scale
        )
        key_grad = (
            key_grad
            + jnp.einsum("gqk,gqd->gkd", grad_scores, query_blk, preferred_element_type=jnp.float32)
            * score_scale
        )
        value_grad = value_grad + jnp.einsum(
            "gqk,gqd->gkd",
            attn_probs.astype(jnp.bfloat16),
            grad_blk,
            preferred_element_type=jnp.float32,
        )
        return ((key_grad, value_grad), query_grad)

    empty = jnp.zeros((head_count, seq_len, head_width), jnp.float32)
    (key_grad, value_grad), query_grad = lax.scan(
        one_block, (empty, empty), jnp.arange(block_count)
    )
    query_grad = query_grad.transpose(1, 0, 2, 3).reshape(head_count, seq_len, head_width)
    return jnp.stack([query_grad, key_grad, value_grad]).astype(jnp.bfloat16)


def token_sum(left, right):
    return jnp.einsum("ti,to->io", left, right, preferred_element_type=jnp.float32)


def back_product(grad_rows, weight):
    return jnp.einsum("to,io->ti", grad_rows, weight, preferred_element_type=jnp.float32)


def local(
    inputs,
    cotangent,
    qkv_weight,
    qkv_first,
    qkv_second,
    out_weight,
    out_first,
    out_second,
    fc_weight,
    fc_first,
    fc_second,
    proj_weight,
    proj_first,
    proj_second,
    vectors,
    vector_first,
    vector_second,
):
    branch = DEPTH ** (-0.5)
    seq_parts = lax.axis_size("seq")
    seq_count, part_len, features = inputs.shape
    tok_rows = seq_count * part_len
    seq_len = part_len * seq_parts
    head_groups = HEADS // seq_parts
    group_width = head_groups * HEAD_DIM
    low_qkv = qkv_weight.astype(jnp.bfloat16)
    low_out = out_weight.astype(jnp.bfloat16)
    low_fc = fc_weight.astype(jnp.bfloat16)
    low_proj = proj_weight.astype(jnp.bfloat16)
    low_vec = vectors.astype(jnp.bfloat16)
    wide_qkv, wide_out, wide_fc, wide_proj, wide_vec = (
        lax.all_gather(low_qkv, "dp", axis=1, tiled=True),
        lax.all_gather(low_out, "dp", axis=1, tiled=True),
        lax.all_gather(low_fc, "dp", axis=1, tiled=True),
        lax.all_gather(low_proj, "dp", axis=1, tiled=True),
        lax.all_gather(low_vec, "dp", axis=1, tiled=True),
    )
    w_qkv, w_out, w_fc, w_proj, w_vec = (
        lax.all_gather(wide_qkv, "seq", axis=0, tiled=True),
        lax.all_gather(wide_out, "seq", axis=0, tiled=True),
        lax.all_gather(wide_fc, "seq", axis=0, tiled=True),
        lax.all_gather(wide_proj, "seq", axis=0, tiled=True),
        lax.all_gather(wide_vec, "seq", axis=0, tiled=True),
    )
    vec_used = w_vec.astype(jnp.float32)
    tokens_in = inputs.astype(jnp.float32).reshape(tok_rows, features)
    h_one = layer_norm(tokens_in, vec_used[0], vec_used[1]).astype(jnp.bfloat16)
    qkv_bias = jnp.concatenate([vec_used[2], jnp.zeros_like(vec_used[2]), vec_used[3]])
    qkv_rows = (jnp.dot(h_one, w_qkv, preferred_element_type=jnp.float32) + qkv_bias).astype(
        jnp.bfloat16
    )
    outgoing = qkv_rows.reshape(seq_count, part_len, 3, seq_parts, group_width)
    arrived = lax.all_to_all(outgoing, "seq", split_axis=3, concat_axis=1, tiled=True)
    heads_all = arrived.reshape(seq_count, seq_len, 3, head_groups, HEAD_DIM).transpose(
        2, 0, 3, 1, 4
    )
    attn_heads, log_total = lax.map(
        lambda items: attend_forward(items[0], items[1], items[2]),
        (heads_all[0], heads_all[1], heads_all[2]),
    )
    leaving = attn_heads.transpose(0, 2, 1, 3).reshape(seq_count, seq_len, 1, group_width)
    returned = lax.all_to_all(leaving, "seq", split_axis=1, concat_axis=2, tiled=True)
    attn_rows = returned.reshape(tok_rows, features)
    attn_out = jnp.dot(attn_rows, w_out, preferred_element_type=jnp.float32) + vec_used[4]
    middle = tokens_in + branch * attn_out
    h_two = layer_norm(middle, vec_used[5], vec_used[6]).astype(jnp.bfloat16)
    hidden = jnp.dot(h_two, w_fc, preferred_element_type=jnp.float32) + vec_used[8:].reshape(-1)
    active = gelu_tanh(hidden).astype(jnp.bfloat16)
    mlp_out = jnp.dot(active, w_proj, preferred_element_type=jnp.float32) + vec_used[7]
    outputs = (middle + branch * mlp_out).astype(jnp.bfloat16).reshape(inputs.shape)
    back_qkv, back_out, back_fc, back_proj = (w_qkv, w_out, w_fc, w_proj)
    grad_out = cotangent.astype(jnp.float32).reshape(tok_rows, features)
    grad_mlp = (branch * grad_out).astype(jnp.bfloat16)
    grad_proj = token_sum(active, grad_mlp)
    grad_proj_bias = jnp.sum(grad_mlp.astype(jnp.float32), 0)
    grad_active = back_product(grad_mlp, back_proj)
    gelu_value, gelu_pull = jax.vjp(gelu_tanh, hidden)
    grad_hidden = gelu_pull(grad_active)[0].astype(jnp.bfloat16)
    grad_fc = token_sum(h_two, grad_hidden)
    grad_fc_bias = jnp.sum(grad_hidden.astype(jnp.float32), 0)
    grad_norm_two = back_product(grad_hidden, back_fc)
    norm_value, norm_pull = jax.vjp(layer_norm, middle, vec_used[5], vec_used[6])
    grad_mid_norm, grad_gain_two, grad_shift_two = norm_pull(grad_norm_two)
    grad_middle = grad_out + grad_mid_norm
    grad_attn_out = (branch * grad_middle).astype(jnp.bfloat16)
    grad_outproj = token_sum(attn_rows, grad_attn_out)
    grad_out_bias = jnp.sum(grad_attn_out.astype(jnp.float32), 0)
    grad_attn = back_product(grad_attn_out, back_out).astype(jnp.bfloat16)
    sending = grad_attn.reshape(seq_count, part_len, seq_parts, group_width)
    grad_arrived = lax.all_to_all(sending, "seq", split_axis=2, concat_axis=1, tiled=True)
    grad_heads = grad_arrived.reshape(seq_count, seq_len, head_groups, HEAD_DIM).transpose(
        0, 2, 1, 3
    )
    grad_qkv_heads = lax.map(
        lambda items: attend_backward(items[0], items[1], items[2], items[3], items[4]),
        (heads_all[0], heads_all[1], heads_all[2], grad_heads, log_total),
    )
    back_leaving = grad_qkv_heads.transpose(0, 3, 1, 2, 4).reshape(
        seq_count, seq_len, 3, 1, group_width
    )
    back_rows = lax.all_to_all(back_leaving, "seq", split_axis=1, concat_axis=3, tiled=True)
    grad_qkv = back_rows.reshape(tok_rows, 3 * features)
    grad_qkv_weight = token_sum(h_one, grad_qkv)
    qkv_sums = jnp.sum(grad_qkv.astype(jnp.float32), 0)
    grad_norm_one = back_product(grad_qkv, back_qkv)
    first_value, first_pull = jax.vjp(layer_norm, tokens_in, vec_used[0], vec_used[1])
    grad_in_norm, grad_gain_one, grad_shift_one = first_pull(grad_norm_one)
    input_grad = (grad_middle + grad_in_norm).astype(jnp.bfloat16).reshape(inputs.shape)
    grad_vec = jnp.concatenate(
        [
            jnp.stack(
                [
                    grad_gain_one,
                    grad_shift_one,
                    qkv_sums[:features],
                    qkv_sums[2 * features :],
                    grad_out_bias,
                    grad_gain_two,
                    grad_shift_two,
                    grad_proj_bias,
                ]
            ),
            grad_fc_bias.reshape(-1, features),
        ],
        0,
    )
    part_qkv, part_out, part_fc, part_proj, part_vec = (
        lax.psum_scatter(grad_qkv_weight, "dp", scatter_dimension=1, tiled=True),
        lax.psum_scatter(grad_outproj, "dp", scatter_dimension=1, tiled=True),
        lax.psum_scatter(grad_fc, "dp", scatter_dimension=1, tiled=True),
        lax.psum_scatter(grad_proj, "dp", scatter_dimension=1, tiled=True),
        lax.psum_scatter(grad_vec, "dp", scatter_dimension=1, tiled=True),
    )
    sum_qkv, sum_out, sum_fc, sum_proj, sum_vec = (
        lax.psum_scatter(
            part_qkv.astype(jnp.bfloat16), "seq", scatter_dimension=0, tiled=True
        ).astype(jnp.float32),
        lax.psum_scatter(
            part_out.astype(jnp.bfloat16), "seq", scatter_dimension=0, tiled=True
        ).astype(jnp.float32),
        lax.psum_scatter(
            part_fc.astype(jnp.bfloat16), "seq", scatter_dimension=0, tiled=True
        ).astype(jnp.float32),
        lax.psum_scatter(
            part_proj.astype(jnp.bfloat16), "seq", scatter_dimension=0, tiled=True
        ).astype(jnp.float32),
        lax.psum_scatter(
            part_vec.astype(jnp.bfloat16), "seq", scatter_dimension=0, tiled=True
        ).astype(jnp.float32),
    )
    qkv_new = adam_update(qkv_weight, qkv_first, qkv_second, sum_qkv, D ** (-0.5), matrix_decay)
    out_new = adam_update(
        out_weight, out_first, out_second, sum_out, max(1, 16 * D // LEN) ** (-0.5), matrix_decay
    )
    fc_new = adam_update(fc_weight, fc_first, fc_second, sum_fc, D ** (-0.5), matrix_decay)
    proj_new = adam_update(
        proj_weight, proj_first, proj_second, sum_proj, FF ** (-0.5), matrix_decay
    )
    vec_new = adam_update(vectors, vector_first, vector_second, sum_vec, 0.5, 0.0)
    return (
        outputs,
        input_grad,
        qkv_new[0],
        qkv_new[1],
        qkv_new[2],
        qkv_new[3],
        out_new[0],
        out_new[1],
        out_new[2],
        out_new[3],
        fc_new[0],
        fc_new[1],
        fc_new[2],
        fc_new[3],
        proj_new[0],
        proj_new[1],
        proj_new[2],
        proj_new[3],
        vec_new[0],
        vec_new[1],
        vec_new[2],
        vec_new[3],
    )


def solution(mesh):
    return jax.shard_map(
        local,
        mesh=mesh,
        in_specs=(
            P("dp", "seq", None),
            P("dp", "seq", None),
            P("seq", "dp"),
            P("seq", "dp"),
            P("seq", "dp"),
            P("seq", "dp"),
            P("seq", "dp"),
            P("seq", "dp"),
            P("seq", "dp"),
            P("seq", "dp"),
            P("seq", "dp"),
            P("seq", "dp"),
            P("seq", "dp"),
            P("seq", "dp"),
            P("seq", "dp"),
            P("seq", "dp"),
            P("seq", "dp"),
        ),
        out_specs=(
            P("dp", "seq", None),
            P("dp", "seq", None),
            P("seq", "dp"),
            P("seq", "dp"),
            P("seq", "dp"),
            P("seq", "dp"),
            P("seq", "dp"),
            P("seq", "dp"),
            P("seq", "dp"),
            P("seq", "dp"),
            P("seq", "dp"),
            P("seq", "dp"),
            P("seq", "dp"),
            P("seq", "dp"),
            P("seq", "dp"),
            P("seq", "dp"),
            P("seq", "dp"),
            P("seq", "dp"),
            P("seq", "dp"),
            P("seq", "dp"),
            P("seq", "dp"),
            P("seq", "dp"),
        ),
        check_vma=False,
    )
```

profile of v0, /device:TPU:0, one launch (start us, length us, event | category | flops | bytes accessed | tf_op | source)
XLA Modules:
  0.0 1290.6 jit_solution(14631618596200599561)
XLA Ops:
  9.1 35.4 %all_gather.32 = bf16[192,2304]{0,1:T(8,128)(2,1)S(1)} all-gather(bf16[192,288]{0,1:T(8,128)(2,1)S(1)} %convert_element_type.140), channel_id=1, replica_groups=mesh['dp'=8,'seq'=4] {'dp'}, dimensions={1}, use_global_device_ids=true | all-gather | bytes 995328 | tf_op jit(solution)/shard_map/all_gather | solution.py:159
  47.4 31.1 %all_gather.34 = bf16[192,768]{0,1:T(8,128)(2,1)S(1)} all-gather(bf16[192,96]{0,1:T(8,128)(2,1)S(1)} %convert_element_type.142), channel_id=1, replica_groups=mesh['dp'=8,'seq'=4] {'dp'}, dimensions={1}, use_global_device_ids=true | all-gather | bytes 331776 | tf_op jit(solution)/shard_map/all_gather | solution.py:160
  79.4 20.3 %all-gather = bf16[8,96,3]{1,2,0:T(4,128)(2,1)S(1)} all-gather(bf16[1,96,3]{1,2,0:T(4,128)(2,1)S(1)} %convert_bitcast_fusion.4), channel_id=1, replica_groups=mesh['dp'=8,'seq'=4] {'dp'}, dimensions={0}, use_global_device_ids=true | all-gather | bytes 5184 | tf_op jit(solution)/shard_map/all_gather | solution.py:163
  121.8 34.2 %all-to-all-done = bf16[1,512,3,4,192]{1,4,2,0,3:T(8,128)(2,1)S(1)} async-done(((bf16[1,512,3,4,192]{1,4,2,0,3:T(8,128)(2,1)}), bf16[1,512,3,4,192]{1,4,2,0,3:T(8,128)(2,1)S(1)}, u32[]{:S(2)}, u32[]{:S(2)}) %all-to-all-start) | async-done | bytes 2359328 | tf_op jit(solution)/shard_map/all_to_all | solution.py:180
  167.1 87.8 %while.46 = (s32[]{:T(128)}, bf16[4,3,512,64]{2,3,1,0:T(8,128)(2,1)}, f32[4,3,512,1]{2,1,3,0:T(4,128)S(1)}, s32[4]{0:T(128)S(1)}, bf16[3,2048,64]{1,2,0:T(8,128)...) while((s32[]{:T(128)}, ...), condition=%wide.region_5.6_spmd.clone, body=%wide.region_2.5_spmd.clone.sunk | while | flops 844200960 | bytes 43968700 | solution.py:63
  264.5 12.7 reduce.19
  283.2 11.5 all-to-all-done.1
  326.1 159.5 %reduce-scatter.24.cloned.1.call-done = f32[3072,96]{0,1:T(8,128)} async-done(((f32[3072,768]{0,1:T(8,128)}), f32[3072,96]{0,1:T(8,128)}) %reduce-scatter.24.cloned.1.call-update) | async-done | bytes 1179664 | tf_op jit(solution)/shard_map/reduce_scatter | solution.py:258
  487.9 21.9 %reduce-scatter.26.cloned.1.call-done = bf16[768,96]{0,1:T(8,128)(2,1)} async-done(((bf16[3072,96]{0,1:T(8,128)(2,1)}), bf16[768,96]{0,1:T(8,128)(2,1)}) %reduce-scatter.26.cloned.1.call-update) | async-done | bytes 147472 | tf_op jit(solution)/shard_map/reduce_scatter | solution.py:271
  512.4 41.2 %all-gather.17.cloned.1.call-done = bf16[768,768]{0,1:T(8,128)(2,1)} async-done(((bf16[768,96]{0,1:T(8,128)(2,1)}), bf16[768,768]{0,1:T(8,128)(2,1)}) %all-gather.17.cloned.1.call-update) | async-done | bytes 1179664 | tf_op jit(solution)/shard_map/all_gather | solution.py:162
  553.6 37.8 %all-gather.19.cloned.1.call-done = bf16[3072,768]{0,1:T(8,128)(2,1)} async-done(((bf16[768,768]{0,1:T(8,128)(2,1)}), bf16[3072,768]{0,1:T(8,128)(2,1)}) %all-gather.19.cloned.1.call-update) | async-done | bytes 4718608 | tf_op jit(solution)/shard_map/all_gather | solution.py:169
  591.5 10.6 convert_reduce_fusion
  622.1 7.8 all-to-all-done.2
  634.3 138.9 %while.47 = (s32[]{:T(128)}, f32[3,2048,64]{1,2,0:T(8,128)}, f32[3,2048,64]{1,2,0:T(8,128)}, bf16[4,3,512,64]{2,3,1,0:T(8,128)(2,1)}, s32[4]{0:T(128)S(1)}, /*in...) while((s32[]{:T(128)}, f32[3,2048,64]{1,2,0:T(8,128)}, ...), condition=%wide.region_12.13_spmd.clone, body=%wide.region_10.12_spmd.clone.sunk | while | flops 2063563776 | bytes 219593376 | solution.py:112
  639.9 7.4 multiply_reduce_fusion.5
  782.4 53.9 %all_to_all.60 = bf16[1,2048,3,1,192]{4,2,3,0,1:T(4,128)(2,1)} all-to-all(bf16[1,2048,3,1,192]{4,2,3,0,1:T(4,128)(2,1)} %copy.188), channel_id=1, replica_groups=mesh['dp'=8,'seq'=4] {'seq'}, dimensions={1} | all-to-all | bytes 4718592 | tf_op jit(solution)/shard_map/all_to_all | solution.py:228
  851.4 9.0 fusion.93
  875.9 104.0 %reduce-scatter.16.cloned.1.call-done = f32[768,288]{0,1:T(8,128)} async-done(((f32[768,2304]{0,1:T(8,128)}), f32[768,288]{0,1:T(8,128)}) %reduce-scatter.16.cloned.1.call-update) | async-done | bytes 884752 | tf_op jit(solution)/shard_map/reduce_scatter | solution.py:255
  982.4 9.1 fusion.63
  991.5 155.0 %reduce-scatter.20.cloned.1.call-done = f32[768,384]{1,0:T(8,128)} async-done(((f32[768,3072]{1,0:T(8,128)}), f32[768,384]{1,0:T(8,128)}) %reduce-scatter.20.cloned.1.call-update) | async-done | bytes 1179664 | tf_op jit(solution)/shard_map/reduce_scatter | solution.py:257
  1151.8 58.6 %reduce-scatter.32.cloned.1.call-done = f32[96,12]{1,0:T(8,128)} async-done(((f32[768,12]{1,0:T(8,128)}), f32[96,12]{1,0:T(8,128)}) %reduce-scatter.32.cloned.1.call-update) | async-done | bytes 4624
  1218.3 14.1 %reduce-scatter.30.cloned.1.call-done = bf16[192,96]{1,0:T(8,128)(2,1)} async-done(((bf16[768,96]{1,0:T(8,128)(2,1)}), bf16[192,96]{1,0:T(8,128)(2,1)}) %reduce-scatter.30.cloned.1.call-update) | async-done | bytes 36880
  1237.3 19.7 %reduce-scatter.28.cloned.1.call-done = bf16[192,288]{1,0:T(8,128)(2,1)} async-done(((bf16[768,288]{1,0:T(8,128)(2,1)}), bf16[192,288]{1,0:T(8,128)(2,1)}) %reduce-scatter.28.cloned.1.call-update) | async-done | bytes 110608
  1262.7 18.9 %reduce-scatter.22.cloned.1.call-done = bf16[192,384]{1,0:T(8,128)(2,1)} async-done(((bf16[768,384]{1,0:T(8,128)(2,1)}), bf16[192,384]{1,0:T(8,128)(2,1)}) %reduce-scatter.22.cloned.1.call-update) | async-done | bytes 147472 | tf_op jit(solution)/shard_map/reduce_scatter | solution.py:268
  (459 shorter events, 394.2 us)
Async XLA Ops:
  7.2 99.6 %all-gather.9.cloned.1.call-start = ((), (), s32[]{:S(2)}) async-start(), calls=%async_computation.13 | async-start | bytes 4423680 | tf_op jit(solution)/shard_map/all_gather | solution.py:166
  45.8 75.4 %all-gather.13.cloned.1.call-start = ((), (), s32[]{:S(2)}) async-start(), calls=%async_computation.15 | async-start | bytes 1327104 | tf_op jit(solution)/shard_map/all_gather | solution.py:161
  46.6 261.9 %all-gather.11.cloned.1.call-start = ((), (), s32[]{:S(2)}) async-start(), calls=%async_computation.14 | async-start | bytes 1474560 | tf_op jit(solution)/shard_map/all_gather | solution.py:167
  117.5 38.4 %all-to-all-start = ((bf16[1,512,3,4,192]{1,4,2,0,3:T(8,128)(2,1)}), bf16[1,512,3,4,192]{1,4,2,0,3:T(8,128)(2,1)S(1)}, u32[]{:S(2)}, u32[]{:S(2)}) async-start(bf16[1,512,3,4,192]{1,4,2,0,3:T(8,128)(2,1)} %copy.176), calls=%async_computation | async-start | bytes 4718592 | tf_op jit(solution)/shard_map/all_to_all | solution.py:180
  121.2 191.3 %all-gather.15.cloned.1.call-start = ((), (), s32[]{:S(2)}) async-start(), calls=%async_computation.16 | async-start | bytes 5898240 | tf_op jit(solution)/shard_map/all_gather | solution.py:168
  279.6 15.1 %all-to-all-start.1 = ((bf16[4,2,49152]{2,1,0:T(2,128)(2,1)}), bf16[4,2,49152]{2,1,0:T(2,128)(2,1)S(1)}, u32[]{:S(2)}, u32[]{:S(2)}) async-start(bf16[4,2,49152]{2,1,0:T(2,128)(2,1)} %reshape.401), calls=%async_computation.1 | async-start | bytes 1572864 | tf_op jit(solution)/shard_map/all_to_all | solution.py:189
  283.1 202.6 %reduce-scatter.24.cloned.1.call-start = ((), (), s32[]{:S(2)}) async-start(), calls=%async_computation.23 | async-start | bytes 10616832 | tf_op jit(solution)/shard_map/reduce_scatter | solution.py:258
  283.1 308.3 %copy-start.55 = (f32[3072]{0:T(1024)}, f32[3072]{0:T(1024)S(1)}, u32[]{:S(2)}) copy-start(f32[3072]{0:T(1024)S(1)} %add.276) | copy-start | bytes 36868
  311.0 298.1 %copy-start.46 = (f32[512]{0:T(512)}, f32[512]{0:T(512)S(1)}, u32[]{:S(2)}) copy-start(f32[512]{0:T(512)S(1)} %broadcast_multiply_fusion) | copy-start | bytes 6148
  312.5 296.7 %copy-start.58 = (f32[512]{0:T(512)}, f32[512]{0:T(512)S(1)}, u32[]{:S(2)}) copy-start(f32[512]{0:T(512)S(1)} %fusion.89) | copy-start | bytes 6148
  326.1 183.7 %reduce-scatter.26.cloned.1.call-start = ((), (), s32[]{:S(2)}) async-start(), calls=%async_computation.24 | async-start | bytes 737280 | tf_op jit(solution)/shard_map/reduce_scatter | solution.py:271
  487.8 65.8 %all-gather.17.cloned.1.call-start = ((), (), s32[]{:S(2)}) async-start(), calls=%async_computation.17 | async-start | bytes 1327104 | tf_op jit(solution)/shard_map/all_gather | solution.py:162
  512.4 79.1 %all-gather.19.cloned.1.call-start = ((), (), s32[]{:S(2)}) async-start(), calls=%async_computation.18 | async-start | bytes 5898240 | tf_op jit(solution)/shard_map/all_gather | solution.py:169
  614.9 15.1 %all-to-all-start.2 = ((bf16[1,512,4,192]{1,3,0,2:T(8,128)(2,1)}), bf16[1,512,4,192]{1,3,0,2:T(8,128)(2,1)S(1)}, u32[]{:S(2)}, u32[]{:S(2)}) async-start(bf16[1,512,4,192]{1,3,0,2:T(8,128)(2,1)} %bitcast.202), calls=%async_computation.2 | async-start | bytes 1572864 | tf_op jit(solution)/shard_map/all_to_all | solution.py:217
  618.4 251.2 %reduce-scatter.18.cloned.1.call-start = ((), (), s32[]{:S(2)}) async-start(), calls=%async_computation.20 | async-start | bytes 2654208 | tf_op jit(solution)/shard_map/reduce_scatter | solution.py:256
  622.1 357.9 %reduce-scatter.16.cloned.1.call-start = ((), (), s32[]{:S(2)}) async-start(), calls=%async_computation.19 | async-start | bytes 7962624 | tf_op jit(solution)/shard_map/reduce_scatter | solution.py:255
  850.7 295.8 %reduce-scatter.20.cloned.1.call-start = ((), (), s32[]{:S(2)}) async-start(), calls=%async_computation.21 | async-start | bytes 10616832 | tf_op jit(solution)/shard_map/reduce_scatter | solution.py:257
  860.4 350.0 %reduce-scatter.32.cloned.1.call-start = ((), (), s32[]{:S(2)}) async-start(), calls=%async_computation.27 | async-start | bytes 442368
  869.5 362.9 %reduce-scatter.30.cloned.1.call-start = ((), (), s32[]{:S(2)}) async-start(), calls=%async_computation.26 | async-start | bytes 245760
  871.4 110.9 %copy-start.61 = (f32[768]{0:T(1024)S(1)}, f32[768]{0:T(1024)}, u32[]{:S(2)}) copy-start(f32[768]{0:T(1024)} %get-tuple-element.359) | copy-start | bytes 9220
  871.4 385.6 %reduce-scatter.28.cloned.1.call-start = ((), (), s32[]{:S(2)}) async-start(), calls=%async_computation.25 | async-start | bytes 737280
  982.3 299.3 %reduce-scatter.22.cloned.1.call-start = ((), (), s32[]{:S(2)}) async-start(), calls=%async_computation.22 | async-start | bytes 737280 | tf_op jit(solution)/shard_map/reduce_scatter | solution.py:268
  991.4 157.3 %copy-start.8 = (f32[512,768]{1,0:T(8,128)S(1)}, f32[512,768]{1,0:T(8,128)}, u32[]{:S(2)}) copy-start(f32[512,768]{1,0:T(8,128)} %copy-done.7) | copy-start | bytes 4718596
  991.4 157.3 %copy-start.19 = (bf16[1,512,768]{2,1,0:T(8,128)(2,1)S(1)}, bf16[1,512,768]{2,1,0:T(8,128)(2,1)}, u32[]{:S(2)}) copy-start(bf16[1,512,768]{2,1,0:T(8,128)(2,1)} %param.22) | copy-start | bytes 2359300
  (112 other events, 1152.6 us)
Sparse Core Ops, SparseCore 0:
  45.9 31.3 all-gather.8
  79.9 40.8 all-gather.12
  123.0 22.7 all-gather.10
  147.2 37.4 all-gather.14
  326.2 159.4 reduce-scatter.23
  488.6 21.1 reduce-scatter.25
  512.5 41.0 all-gather.16
  555.2 36.2 all-gather.18
  622.7 70.4 reduce-scatter.17
  850.8 129.1 reduce-scatter.15
  984.0 162.4 reduce-scatter.19
  1149.9 60.4 reduce-scatter.31
  1213.6 18.7 reduce-scatter.29
  1234.9 22.0 reduce-scatter.27
  1259.5 22.0 reduce-scatter.21
where the time goes:
time: 1300 us; the launch traced here: 1290 us
  waiting for transfers between devices  685 us (53%)
  matrix products  217 us (17%)
  blocking collectives  151 us (12%)
  local copies, waits for them, and re-layouts  102 us (8%)
  other arithmetic  100 us (8%)
  between operations  15.9 us (1%)
    reduce_scatter x1, waiting for transfers between devices, local(): lax.psum_scatter(grad_proj, 'dp', scatter_dimension=1, tiled=True)  160 us
    reduce_scatter x1, waiting for transfers between devices, local(): lax.psum_scatter(grad_fc, 'dp', scatter_dimension=1, tiled=True)  155 us
    reduce_scatter x1, waiting for transfers between devices, local(): lax.psum_scatter(grad_qkv_weight, 'dp', scatter_dimension=1, tiled=True)  104 us
    unnamed x18, waiting for transfers between devices  93.2 us
    all_to_all x1, blocking collectives, local(): lax.all_to_all(back_leaving, 'seq', split_axis=1, concat_axis=3, tiled=True)  53.9 us
    all_gather x1, waiting for transfers between devices, local(): lax.all_gather(low_proj, 'dp', axis=1, tiled=True)  41.2 us
    all_gather x1, waiting for transfers between devices, local(): lax.all_gather(wide_proj, 'seq', axis=0, tiled=True)  37.8 us
    all_gather x1, blocking collectives, local(): lax.all_gather(low_qkv, 'dp', axis=1, tiled=True)  35.4 us
  transfers between devices with their start and end apart: 18, of which 13 were waited for; matrix products, arithmetic and copies ran while one was open for 28% of the time, Pallas kernels for 0%

commit v1 on v0

--- a/solution.py
+++ b/solution.py
@@ -2,6 +2,7 @@
 import jax.numpy as jnp
 from jax import lax
 from jax.sharding import PartitionSpec as P
+from jax.lax import axis_index, axis_size, ppermute
 
 D = 768
 HEADS = 12
@@ -13,6 +14,23 @@
 beta_one = 0.5
 beta_two = 0.5
 matrix_decay = 0.1
+
+
+def touch_screen(inner_x, a_name, dim_at):
+    clean = axis_size(a_name)
+    d_next = axis_index(a_name)
+    piece_now, spare = (clean, d_next)
+    a_next, built = (inner_x, 1)
+    while built < piece_now:
+        all_rows = []
+        for dd in [*range(piece_now)]:
+            all_rows.append((dd, dd ^ built))
+        oldest = ppermute(a_next, axis_name=a_name, perm=all_rows)
+        met_up = jnp.concatenate([a_next, oldest], dim_at)
+        answer = jnp.concatenate([oldest, a_next], dim_at)
+        a_next = jnp.where(spare & built == 0, met_up, answer)
+        built = 2 * built
+    return a_next
 
 
 def layer_norm(values, gain, shift):
@@ -166,7 +184,7 @@
         lax.all_gather(wide_qkv, "seq", axis=0, tiled=True),
         lax.all_gather(wide_out, "seq", axis=0, tiled=True),
         lax.all_gather(wide_fc, "seq", axis=0, tiled=True),
-        lax.all_gather(wide_proj, "seq", axis=0, tiled=True),
+        touch_screen(wide_proj, "seq", 0),
         lax.all_gather(wide_vec, "seq", axis=0, tiled=True),
     )
     vec_used = w_vec.astype(jnp.float32)

time: 1300 us -> 1320 us (1.015)
  waiting for transfers between devices: 685 us -> 699 us
    ppermute x0 -> x2, waiting for transfers between devices: none -> 55.3 us  [touch_screen(): oldest = ppermute(a_next, axis_name=a_name, perm=all_rows)]
    all_gather x1 -> x0, waiting for transfers between devices: 37.8 us -> none  [local(): lax.all_gather(wide_proj, 'seq', axis=0, tiled=True)]
    unnamed x18 -> x17, waiting for transfers between devices: 93.2 us -> 93.2 us
  transfers between devices with their start and end apart: 18 -> 19, of which waited for: 13 -> 14; matrix products, arithmetic and copies ran while one was open for 28% -> 28% of each run, Pallas kernels for 0% -> 0%
where the time goes in v1:
time: 1320 us; the launch traced here: 1310 us
  waiting for transfers between devices  699 us (53%)
  matrix products  221 us (17%)
  blocking collectives  151 us (11%)
  other arithmetic  104 us (8%)
  local copies, waits for them, and re-layouts  102 us (8%)
  between operations  15.7 us (1%)
    reduce_scatter x1, waiting for transfers between devices, local(): lax.psum_scatter(grad_proj, 'dp', scatter_dimension=1, tiled=True)  160 us
    reduce_scatter x1, waiting for transfers between devices, local(): lax.psum_scatter(grad_fc, 'dp', scatter_dimension=1, tiled=True)  153 us
    reduce_scatter x1, waiting for transfers between devices, local(): lax.psum_scatter(grad_qkv_weight, 'dp', scatter_dimension=1, tiled=True)  102 us
    unnamed x17, waiting for transfers between devices  93.2 us
    ppermute x2, waiting for transfers between devices, touch_screen(): oldest = ppermute(a_next, axis_name=a_name, perm=all_rows)  55.3 us
    all_to_all x1, blocking collectives, local(): lax.all_to_all(back_leaving, 'seq', split_axis=1, concat_axis=3, tiled=True)  53.9 us
    all_gather x1, waiting for transfers between devices, local(): lax.all_gather(low_proj, 'dp', axis=1, tiled=True)  41.3 us
    all_gather x1, blocking collectives, local(): lax.all_gather(low_qkv, 'dp', axis=1, tiled=True)  35.4 us
  transfers between devices with their start and end apart: 19, of which 14 were waited for; matrix products, arithmetic and copies ran while one was open for 28% of the time, Pallas kernels for 0%

profile of v1, /device:TPU:0, one launch (start us, length us, event | category | flops | bytes accessed | tf_op | source)
XLA Modules:
  0.0 1313.4 jit_solution(2982157891912748607)
XLA Ops:
  9.1 35.4 %all_gather.29 = bf16[192,2304]{0,1:T(8,128)(2,1)S(1)} all-gather(bf16[192,288]{0,1:T(8,128)(2,1)S(1)} %convert_element_type.140), channel_id=1, replica_groups=mesh['dp'=8,'seq'=4] {'dp'}, dimensions={1}, use_global_device_ids=true | all-gather | bytes 995328 | tf_op jit(solution)/shard_map/all_gather | solution.py:177
  47.4 31.1 %all_gather.31 = bf16[192,768]{0,1:T(8,128)(2,1)S(1)} all-gather(bf16[192,96]{0,1:T(8,128)(2,1)S(1)} %convert_element_type.142), channel_id=1, replica_groups=mesh['dp'=8,'seq'=4] {'dp'}, dimensions={1}, use_global_device_ids=true | all-gather | bytes 331776 | tf_op jit(solution)/shard_map/all_gather | solution.py:178
  79.4 20.3 %all-gather = bf16[8,96,3]{1,2,0:T(4,128)(2,1)S(1)} all-gather(bf16[1,96,3]{1,2,0:T(4,128)(2,1)S(1)} %convert_bitcast_fusion.4), channel_id=1, replica_groups=mesh['dp'=8,'seq'=4] {'dp'}, dimensions={0}, use_global_device_ids=true | all-gather | bytes 5184 | tf_op jit(solution)/shard_map/all_gather | solution.py:181
  121.7 34.2 %all-to-all-done = bf16[1,512,3,4,192]{1,4,2,0,3:T(8,128)(2,1)S(1)} async-done(((bf16[1,512,3,4,192]{1,4,2,0,3:T(8,128)(2,1)}), bf16[1,512,3,4,192]{1,4,2,0,3:T(8,128)(2,1)S(1)}, u32[]{:S(2)}, u32[]{:S(2)}) %all-to-all-start) | async-done | bytes 2359328 | tf_op jit(solution)/shard_map/all_to_all | solution.py:198
  167.2 87.8 %while.46 = (s32[]{:T(128)}, bf16[4,3,512,64]{2,3,1,0:T(8,128)(2,1)}, f32[4,3,512,1]{2,1,3,0:T(4,128)S(1)}, s32[4]{0:T(128)S(1)}, bf16[3,2048,64]{1,2,0:T(8,128)...) while((s32[]{:T(128)}, ...), condition=%wide.region_5.6_spmd.clone, body=%wide.region_2.5_spmd.clone.sunk | while | flops 844200960 | bytes 43968700 | solution.py:81
  264.6 12.7 reduce.19
  283.2 11.5 all-to-all-done.1
  326.2 159.5 %reduce-scatter.24.cloned.1.call-done = f32[3072,96]{0,1:T(8,128)} async-done(((f32[3072,768]{0,1:T(8,128)}), f32[3072,96]{0,1:T(8,128)}) %reduce-scatter.24.cloned.1.call-update) | async-done | bytes 1179664 | tf_op jit(solution)/shard_map/reduce_scatter | solution.py:276
  488.0 21.9 %reduce-scatter.26.cloned.1.call-done = bf16[768,96]{0,1:T(8,128)(2,1)} async-done(((bf16[3072,96]{0,1:T(8,128)(2,1)}), bf16[768,96]{0,1:T(8,128)(2,1)}) %reduce-scatter.26.cloned.1.call-update) | async-done | bytes 147472 | tf_op jit(solution)/shard_map/reduce_scatter | solution.py:289
  512.5 41.3 %all-gather.16.cloned.1.call-done = bf16[768,768]{0,1:T(8,128)(2,1)} async-done(((bf16[768,96]{0,1:T(8,128)(2,1)}), bf16[768,768]{0,1:T(8,128)(2,1)}) %all-gather.16.cloned.1.call-update) | async-done | bytes 1179664 | tf_op jit(solution)/shard_map/all_gather | solution.py:180
  562.4 52.1 %collective-permute-done.1 = bf16[1536,768]{0,1:T(8,128)(2,1)} collective-permute-done((bf16[1536,768]{0,1:T(8,128)(2,1)}, bf16[1536,768]{0,1:T(8,128)(2,1)}, u32[]{:S(2)}, u32[]{:S(2)}) %collective-permute-start.1) | collective-permute-done | bytes 2359328 | tf_op jit(solution)/shard_map/ppermute | solution.py:28
  614.5 12.9 convert_reduce_fusion
  647.5 7.8 all-to-all-done.2
  659.6 139.0 %while.47 = (s32[]{:T(128)}, f32[3,2048,64]{1,2,0:T(8,128)}, f32[3,2048,64]{1,2,0:T(8,128)}, bf16[4,3,512,64]{2,3,1,0:T(8,128)(2,1)}, s32[4]{0:T(128)S(1)}, /*in...) while((s32[]{:T(128)}, f32[3,2048,64]{1,2,0:T(8,128)}, ...), condition=%wide.region_12.13_spmd.clone, body=%wide.region_10.12_spmd.clone.sunk | while | flops 2063563776 | bytes 219593376 | solution.py:130
  665.4 7.3 multiply_reduce_fusion.5
  807.7 53.9 %all_to_all.60 = bf16[1,2048,3,1,192]{4,2,3,0,1:T(4,128)(2,1)} all-to-all(bf16[1,2048,3,1,192]{4,2,3,0,1:T(4,128)(2,1)} %copy.188), channel_id=1, replica_groups=mesh['dp'=8,'seq'=4] {'seq'}, dimensions={1} | all-to-all | bytes 4718592 | tf_op jit(solution)/shard_map/all_to_all | solution.py:246
  876.7 8.9 fusion.93
  901.2 101.9 %reduce-scatter.16.cloned.1.call-done = f32[768,288]{0,1:T(8,128)} async-done(((f32[768,2304]{0,1:T(8,128)}), f32[768,288]{0,1:T(8,128)}) %reduce-scatter.16.cloned.1.call-update) | async-done | bytes 884752 | tf_op jit(solution)/shard_map/reduce_scatter | solution.py:273
  1005.5 10.7 fusion.63
  1016.2 153.2 %reduce-scatter.20.cloned.1.call-done = f32[768,384]{1,0:T(8,128)} async-done(((f32[768,3072]{1,0:T(8,128)}), f32[768,384]{1,0:T(8,128)}) %reduce-scatter.20.cloned.1.call-update) | async-done | bytes 1179664 | tf_op jit(solution)/shard_map/reduce_scatter | solution.py:275
  1174.8 58.7 %reduce-scatter.32.cloned.1.call-done = f32[96,12]{1,0:T(8,128)} async-done(((f32[768,12]{1,0:T(8,128)}), f32[96,12]{1,0:T(8,128)}) %reduce-scatter.32.cloned.1.call-update) | async-done | bytes 4624
  1241.3 14.0 %reduce-scatter.30.cloned.1.call-done = bf16[192,96]{1,0:T(8,128)(2,1)} async-done(((bf16[768,96]{1,0:T(8,128)(2,1)}), bf16[192,96]{1,0:T(8,128)(2,1)}) %reduce-scatter.30.cloned.1.call-update) | async-done | bytes 36880
  1260.2 19.9 %reduce-scatter.28.cloned.1.call-done = bf16[192,288]{1,0:T(8,128)(2,1)} async-done(((bf16[768,288]{1,0:T(8,128)(2,1)}), bf16[192,288]{1,0:T(8,128)(2,1)}) %reduce-scatter.28.cloned.1.call-update) | async-done | bytes 110608
  1285.7 18.9 %reduce-scatter.22.cloned.1.call-done = bf16[192,384]{1,0:T(8,128)(2,1)} async-done(((bf16[768,384]{1,0:T(8,128)(2,1)}), bf16[192,384]{1,0:T(8,128)(2,1)}) %reduce-scatter.22.cloned.1.call-update) | async-done | bytes 147472 | tf_op jit(solution)/shard_map/reduce_scatter | solution.py:286
  (461 shorter events, 402.9 us)
Async XLA Ops:
  7.2 99.6 %all-gather.8.cloned.1.call-start = ((), (), s32[]{:S(2)}) async-start(), calls=%async_computation.13 | async-start | bytes 4423680 | tf_op jit(solution)/shard_map/all_gather | solution.py:184
  45.8 75.4 %all-gather.12.cloned.1.call-start = ((), (), s32[]{:S(2)}) async-start(), calls=%async_computation.15 | async-start | bytes 1327104 | tf_op jit(solution)/shard_map/all_gather | solution.py:179
  46.6 261.9 %all-gather.10.cloned.1.call-start = ((), (), s32[]{:S(2)}) async-start(), calls=%async_computation.14 | async-start | bytes 1474560 | tf_op jit(solution)/shard_map/all_gather | solution.py:185
  117.5 38.4 %all-to-all-start = ((bf16[1,512,3,4,192]{1,4,2,0,3:T(8,128)(2,1)}), bf16[1,512,3,4,192]{1,4,2,0,3:T(8,128)(2,1)S(1)}, u32[]{:S(2)}, u32[]{:S(2)}) async-start(bf16[1,512,3,4,192]{1,4,2,0,3:T(8,128)(2,1)} %copy.176), calls=%async_computation | async-start | bytes 4718592 | tf_op jit(solution)/shard_map/all_to_all | solution.py:198
  121.1 191.4 %all-gather.14.cloned.1.call-start = ((), (), s32[]{:S(2)}) async-start(), calls=%async_computation.16 | async-start | bytes 5898240 | tf_op jit(solution)/shard_map/all_gather | solution.py:186
  279.7 15.1 %all-to-all-start.1 = ((bf16[4,2,49152]{2,1,0:T(2,128)(2,1)}), bf16[4,2,49152]{2,1,0:T(2,128)(2,1)S(1)}, u32[]{:S(2)}, u32[]{:S(2)}) async-start(bf16[4,2,49152]{2,1,0:T(2,128)(2,1)} %reshape.401), calls=%async_computation.1 | async-start | bytes 1572864 | tf_op jit(solution)/shard_map/all_to_all | solution.py:207
  283.2 202.6 %reduce-scatter.24.cloned.1.call-start = ((), (), s32[]{:S(2)}) async-start(), calls=%async_computation.22 | async-start | bytes 10616832 | tf_op jit(solution)/shard_map/reduce_scatter | solution.py:276
  283.2 331.3 %copy-start.55 = (f32[3072]{0:T(1024)}, f32[3072]{0:T(1024)S(1)}, u32[]{:S(2)}) copy-start(f32[3072]{0:T(1024)S(1)} %add.276) | copy-start | bytes 36868
  311.0 323.4 %copy-start.46 = (f32[512]{0:T(512)}, f32[512]{0:T(512)S(1)}, u32[]{:S(2)}) copy-start(f32[512]{0:T(512)S(1)} %broadcast_multiply_fusion) | copy-start | bytes 6148
  312.5 322.0 %copy-start.58 = (f32[512]{0:T(512)}, f32[512]{0:T(512)S(1)}, u32[]{:S(2)}) copy-start(f32[512]{0:T(512)S(1)} %fusion.87) | copy-start | bytes 6148
  326.2 183.7 %reduce-scatter.26.cloned.1.call-start = ((), (), s32[]{:S(2)}) async-start(), calls=%async_computation.23 | async-start | bytes 737280 | tf_op jit(solution)/shard_map/reduce_scatter | solution.py:289
  487.9 65.8 %all-gather.16.cloned.1.call-start = ((), (), s32[]{:S(2)}) async-start(), calls=%async_computation.17 | async-start | bytes 1327104 | tf_op jit(solution)/shard_map/all_gather | solution.py:180
  553.7 3.2 collective-permute-start
  560.9 53.6 %collective-permute-start.1 = (bf16[1536,768]{0,1:T(8,128)(2,1)}, bf16[1536,768]{0,1:T(8,128)(2,1)}, u32[]{:S(2)}, u32[]{:S(2)}) collective-permute-start(bf16[1536,768]{0,1:T(8,128)(2,1)} %maximum_select_fusion.1), channel_id=1, source_target_pairs={{0,2},{1,3},{2,0},{3,1},{4,6},{5,7},{6,4},{7,5},{8,10},{9,11},{10,... | collective-permute-start | bytes 7077896 | tf_op jit(solution)/shard_map/ppermute | solution.py:28
  640.2 15.1 %all-to-all-start.2 = ((bf16[1,512,4,192]{1,3,0,2:T(8,128)(2,1)}), bf16[1,512,4,192]{1,3,0,2:T(8,128)(2,1)S(1)}, u32[]{:S(2)}, u32[]{:S(2)}) async-start(bf16[1,512,4,192]{1,3,0,2:T(8,128)(2,1)} %bitcast.198), calls=%async_computation.2 | async-start | bytes 1572864 | tf_op jit(solution)/shard_map/all_to_all | solution.py:235
  643.7 251.1 %reduce-scatter.18.cloned.1.call-start = ((), (), s32[]{:S(2)}) async-start(), calls=%async_computation.19 | async-start | bytes 2654208 | tf_op jit(solution)/shard_map/reduce_scatter | solution.py:274
  647.5 355.6 %reduce-scatter.16.cloned.1.call-start = ((), (), s32[]{:S(2)}) async-start(), calls=%async_computation.18 | async-start | bytes 7962624 | tf_op jit(solution)/shard_map/reduce_scatter | solution.py:273
  876.0 293.4 %reduce-scatter.20.cloned.1.call-start = ((), (), s32[]{:S(2)}) async-start(), calls=%async_computation.20 | async-start | bytes 10616832 | tf_op jit(solution)/shard_map/reduce_scatter | solution.py:275
  885.7 347.8 %reduce-scatter.32.cloned.1.call-start = ((), (), s32[]{:S(2)}) async-start(), calls=%async_computation.26 | async-start | bytes 442368
  894.8 360.5 %reduce-scatter.30.cloned.1.call-start = ((), (), s32[]{:S(2)}) async-start(), calls=%async_computation.25 | async-start | bytes 245760
  896.7 383.3 %reduce-scatter.28.cloned.1.call-start = ((), (), s32[]{:S(2)}) async-start(), calls=%async_computation.24 | async-start | bytes 737280
  1005.4 299.3 %reduce-scatter.22.cloned.1.call-start = ((), (), s32[]{:S(2)}) async-start(), calls=%async_computation.21 | async-start | bytes 737280 | tf_op jit(solution)/shard_map/reduce_scatter | solution.py:286
  1016.2 155.5 %copy-start.8 = (f32[512,768]{1,0:T(8,128)S(1)}, f32[512,768]{1,0:T(8,128)}, u32[]{:S(2)}) copy-start(f32[512,768]{1,0:T(8,128)} %copy-done.7) | copy-start | bytes 4718596
  1016.2 155.5 %copy-start.19 = (bf16[1,512,768]{2,1,0:T(8,128)(2,1)S(1)}, bf16[1,512,768]{2,1,0:T(8,128)(2,1)}, u32[]{:S(2)}) copy-start(bf16[1,512,768]{2,1,0:T(8,128)(2,1)} %param.22) | copy-start | bytes 2359300
  (113 other events, 1311.3 us)
Sparse Core Ops, SparseCore 0:
  45.9 31.3 all-gather.7
  79.9 40.8 all-gather.11
  123.0 22.7 all-gather.9
  147.2 37.4 all-gather.13
  326.3 159.4 reduce-scatter.23
  488.7 21.1 reduce-scatter.25
  512.7 41.0 all-gather.15
  648.1 68.2 reduce-scatter.17
  876.2 126.8 reduce-scatter.15
  1006.9 162.4 reduce-scatter.19
  1173.0 60.3 reduce-scatter.31
  1236.5 18.7 reduce-scatter.29
  1258.0 22.0 reduce-scatter.27
  1282.6 22.0 reduce-scatter.21
